TPU v7x, 128 devices: a whole 4x4x4 slice. The times are simulated.
128 devices in a mesh: req: 32 (over x, y, core), head: 4 (over z).
Axes of the slice: x: 4, y: 4, z: 4, core: 2. Of those that a mesh axis runs over, the one named last changes fastest.
Arguments:
- prefill_query: bfloat16 [16384, 2048], P('req', 'head'), may hold values from -16 to 16
- prefill_new_pairs: bfloat16 [16384, 2, 1024], P('req', None, 'head'), may hold values from -16 to 16
- prefill_cache: bfloat16 [32, 2, 2048, 1024], P('req', None, None, 'head'), may hold values from -16 to 16
- prefill_start: int32 [32], P('req'), may hold values from 0 to 2048, as said below
- decode_query: bfloat16 [96, 2048], P('req', 'head'), may hold values from -16 to 16
- decode_fresh: bfloat16 [96, 2, 1024], P('req', None, 'head'), may hold values from -16 to 16
- decode_cache: bfloat16 [96, 2, 2048, 1024], P('req', None, None, 'head'), may hold values from -16 to 16
- decode_length: int32 [96], P('req'), may hold values from 2 to 2048
- decode_slot: int32 [96], P('req'), may hold values from 0 to 95, each once
- prefill_states: bfloat16 [16384, 2048], P('req', 'head'), may hold values from -32 to 32
- decode_states: bfloat16 [96, 2048], P('req', 'head'), may hold values from -32 to 32
- output_proj: bfloat16 [2048, 2048], P('head', 'req'), may hold values from -0.125 to 0.125
- norm_gain: bfloat16 [2048], replicated, may hold values from 0.099609375 to 1.8984375
- gate_weight: bfloat16 [2048, 6144], P('req', 'head'), may hold values from -0.125 to 0.125
- up_weight: bfloat16 [2048, 6144], P('req', 'head'), may hold values from -0.125 to 0.125
- down_weight: bfloat16 [6144, 2048], P('head', 'req'), may hold values from -0.078125 to 0.078125
Outputs:
- prefill_result: bfloat16 [16384, 2048], P('req', 'head')
- decode_result: bfloat16 [96, 2048], P('req', 'head')
Inputs may be any that keep to these rules, and one draw needn't show every extreme that they name: `decode_slot`: a permutation; the cache of slot s is held by req index s // 3. `prefill_start`: a multiple of 512.
All inputs are finite; a program needn't handle non-finite values.
Results may differ from a plain program's by a relative error of at most 0.0094.
Values may be sent and summed in bfloat16 or wider, within the bound.
No kernel may reach another device: no remote copies, remote signals or barrier semaphores. Data moves between devices by JAX's collectives and lax.ppermute only.
A program may use at most 128 MiB of HBM per device.

v0:
```python
import math
import jax
import jax.numpy as jnp
from jax import lax
from jax.sharding import PartitionSpec as P

HEAD_SIZE = 128
REQUEST_TOKENS = 512
rope_base = 1000000.0
norm_eps = 1e-06


def rope_tables(positions, head_size):
    half_size = head_size // 2
    lane_index = jnp.arange(half_size, dtype=jnp.float32)
    inverse = jnp.power(jnp.float32(rope_base), -2.0 * lane_index / head_size)
    angles = positions.astype(jnp.float32)[:, None] * inverse[None, :]
    cosine = jnp.concatenate([jnp.cos(angles), jnp.cos(angles)], axis=1)
    sine_table = jnp.concatenate([jnp.sin(angles), jnp.sin(angles)], axis=1)
    return (cosine, sine_table)


def rotate(vectors, cosine, sine_table):
    half_size = vectors.shape[-1] // 2
    front_half = vectors[..., :half_size]
    back_half = vectors[..., half_size:]
    turned = jnp.concatenate([-back_half, front_half], axis=-1)
    return vectors * cosine[:, None, :] + turned * sine_table[:, None, :]


def attend(query_rows, key_rows, value_rows, visible):
    row_count, head_count, head_size = query_rows.shape
    groups = key_rows.shape[1]
    grouped = query_rows.reshape(row_count, groups, head_count // groups, head_size)
    scores = jnp.einsum("qhgd,khd->hgqk", grouped, key_rows, preferred_element_type=jnp.float32) * (
        1.0 / math.sqrt(head_size)
    )
    scores = jnp.where(visible[None, None], scores, -jnp.inf)
    highest = jnp.max(scores, axis=-1, keepdims=True)
    unnormed = jnp.exp(scores - highest)
    totals = jnp.sum(unnormed, axis=-1, keepdims=True)
    rounded = unnormed.astype(jnp.bfloat16)
    blended = jnp.einsum("hgqk,khd->qhgd", rounded, value_rows, preferred_element_type=jnp.float32)
    blended = blended / jnp.transpose(totals, (2, 0, 1, 3))
    return blended.reshape(row_count, head_count * head_size).astype(jnp.bfloat16)


def prefill_task(query_rows, fresh_rows, cache_rows, offset_value, head_size):
    span_len = query_rows.shape[0]
    positions = offset_value + jnp.arange(span_len, dtype=jnp.int32)
    cosine, sine_table = rope_tables(positions, head_size)
    head_count = query_rows.shape[1] // head_size
    groups = fresh_rows.shape[2] // head_size
    rot_query = rotate(
        query_rows.astype(jnp.float32).reshape(span_len, head_count, head_size), cosine, sine_table
    ).astype(jnp.bfloat16)
    rot_key = rotate(
        fresh_rows[:, 0].astype(jnp.float32).reshape(span_len, groups, head_size),
        cosine,
        sine_table,
    ).astype(jnp.bfloat16)
    cache_len = cache_rows.shape[1]
    key_rows = jnp.concatenate(
        [cache_rows[0].reshape(cache_len, groups, head_size), rot_key], axis=0
    )
    value_rows = jnp.concatenate(
        [
            cache_rows[1].reshape(cache_len, groups, head_size),
            fresh_rows[:, 1].reshape(span_len, groups, head_size),
        ],
        axis=0,
    )
    cache_seen = jnp.broadcast_to(
        jnp.arange(cache_len, dtype=jnp.int32)[None, :] < offset_value, (span_len, cache_len)
    )
    own_seen = (
        jnp.arange(span_len, dtype=jnp.int32)[None, :]
        <= jnp.arange(span_len, dtype=jnp.int32)[:, None]
    )
    visible = jnp.concatenate([cache_seen, own_seen], axis=1)
    return attend(rot_query, key_rows, value_rows, visible)


def decode_task(query_rows, fresh_rows, cache_rows, length, head_size):
    positions = jnp.reshape(length, (1,))
    cosine, sine_table = rope_tables(positions, head_size)
    head_count = query_rows.shape[0] // head_size
    groups = fresh_rows.shape[1] // head_size
    rot_query = rotate(
        query_rows.astype(jnp.float32).reshape(1, head_count, head_size), cosine, sine_table
    ).astype(jnp.bfloat16)
    rot_key = rotate(
        fresh_rows[0].astype(jnp.float32).reshape(1, groups, head_size), cosine, sine_table
    ).astype(jnp.bfloat16)
    cache_len = cache_rows.shape[1]
    key_rows = jnp.concatenate(
        [cache_rows[0].reshape(cache_len, groups, head_size), rot_key], axis=0
    )
    value_rows = jnp.concatenate(
        [
            cache_rows[1].reshape(cache_len, groups, head_size),
            fresh_rows[1].reshape(1, groups, head_size),
        ],
        axis=0,
    )
    visible = jnp.concatenate(
        [jnp.arange(cache_len, dtype=jnp.int32)[None, :] < length, jnp.ones((1, 1), jnp.bool_)],
        axis=1,
    )
    return attend(rot_query, key_rows, value_rows, visible)[0]


def decode_attend(own_query, own_fresh, decode_cache, decode_length):

    def one_slot(query_rows, fresh_rows, cache_rows, length):
        return decode_task(query_rows, fresh_rows, cache_rows, length, HEAD_SIZE)

    return jax.vmap(one_slot)(own_query, own_fresh, decode_cache, decode_length)


def body(
    prefill_query,
    prefill_new_pairs,
    prefill_cache,
    prefill_start,
    decode_query,
    decode_fresh,
    decode_cache,
    decode_length,
    decode_slot,
    prefill_states,
    decode_states,
    output_proj,
    norm_gain,
    gate_weight,
    up_weight,
    down_weight,
):
    local_prefills = prefill_query.shape[0] // REQUEST_TOKENS
    query_blocks = prefill_query.reshape(local_prefills, REQUEST_TOKENS, prefill_query.shape[1])
    newest_blocks = prefill_new_pairs.reshape(
        local_prefills, REQUEST_TOKENS, 2, prefill_new_pairs.shape[2]
    )
    prefill_att = lax.map(
        lambda operands: prefill_task(
            operands[0], operands[1], operands[2], operands[3], HEAD_SIZE
        ),
        (query_blocks, newest_blocks, prefill_cache, prefill_start),
    )
    prefill_att = prefill_att.reshape(local_prefills * REQUEST_TOKENS, prefill_query.shape[1])
    local_decodes = decode_query.shape[0]
    fresh_width = decode_fresh.shape[2]
    fresh_flat = decode_fresh.reshape(local_decodes, 2 * fresh_width)
    slot_marks = decode_slot.astype(jnp.bfloat16)
    every_query, every_fresh, every_slot = (
        lax.all_gather(decode_query, "req", axis=0, tiled=True),
        lax.all_gather(fresh_flat, "req", axis=0, tiled=True),
        lax.all_gather(slot_marks, "req", axis=0, tiled=True),
    )
    owned = lax.axis_index("req") * local_decodes + jnp.arange(local_decodes, dtype=jnp.int32)
    picker = (every_slot.astype(jnp.int32)[None, :] == owned[:, None]).astype(jnp.bfloat16)
    own_query = jnp.dot(picker, every_query, preferred_element_type=jnp.float32).astype(
        jnp.bfloat16
    )
    own_fresh = jnp.dot(picker, every_fresh, preferred_element_type=jnp.float32).astype(
        jnp.bfloat16
    )
    own_att = decode_attend(
        own_query, own_fresh.reshape(local_decodes, 2, fresh_width), decode_cache, decode_length
    )
    every_att = lax.all_gather(own_att, "req", axis=0, tiled=True)
    total_slots = every_att.shape[0]
    chooser = (decode_slot[:, None] == jnp.arange(total_slots, dtype=jnp.int32)[None, :]).astype(
        jnp.bfloat16
    )
    decode_att = jnp.dot(chooser, every_att, preferred_element_type=jnp.float32).astype(
        jnp.bfloat16
    )
    attended = jnp.concatenate([prefill_att, decode_att], axis=0)
    states = jnp.concatenate([prefill_states, decode_states], axis=0)
    partial_value = jnp.dot(
        attended,
        lax.all_gather(output_proj, "req", axis=1, tiled=True),
        preferred_element_type=jnp.float32,
    )
    model_width = partial_value.shape[1]
    share_cols = model_width // lax.axis_size("head")
    share_start = lax.axis_index("head") * share_cols
    own_block = lax.dynamic_slice_in_dim(partial_value, share_start, share_cols, 1) + states.astype(
        jnp.float32
    )
    placed = lax.dynamic_update_slice_in_dim(partial_value, own_block, share_start, 1)
    summed_full = lax.psum(placed, "head")
    mean_square = jnp.mean(summed_full * summed_full, axis=1, keepdims=True)
    normed = (
        summed_full * lax.rsqrt(mean_square + norm_eps) * norm_gain.astype(jnp.float32)
    ).astype(jnp.bfloat16)
    summed = lax.dynamic_slice_in_dim(summed_full, share_start, share_cols, 1)

    def add_rows(weight_piece):
        return jnp.dot(normed, weight_piece, preferred_element_type=jnp.float32)

    gate_sum = add_rows(lax.all_gather(gate_weight, "req", axis=0, tiled=True))
    upper = add_rows(lax.all_gather(up_weight, "req", axis=0, tiled=True))
    hidden = (jax.nn.silu(gate_sum) * upper).astype(jnp.bfloat16)
    down_terms = jnp.dot(
        hidden,
        lax.all_gather(down_weight, "req", axis=1, tiled=True),
        preferred_element_type=jnp.float32,
    )
    result = (
        summed + lax.psum_scatter(down_terms, "head", scatter_dimension=1, tiled=True)
    ).astype(jnp.bfloat16)
    prefill_rows = prefill_att.shape[0]
    return (result[:prefill_rows], result[prefill_rows:])


def solution(mesh):
    in_specs = (
        P("req", "head"),
        P("req", None, "head"),
        P("req", None, None, "head"),
        P("req"),
        P("req", "head"),
        P("req", None, "head"),
        P("req", None, None, "head"),
        P("req"),
        P("req"),
        P("req", "head"),
        P("req", "head"),
        P("head", "req"),
        P(),
        P("req", "head"),
        P("req", "head"),
        P("head", "req"),
    )
    out_specs = (P("req", "head"), P("req", "head"))
    return jax.shard_map(body, mesh=mesh, in_specs=in_specs, out_specs=out_specs, check_vma=False)
```

profile of v0, /device:TPU:1, one launch (start us, length us, event | category | flops | bytes accessed | tf_op | source)
XLA Modules:
  0.0 560.0 jit_solution(2752393943931964175)
XLA Ops:
  11.5 64.1 %all-reduce.1 = bf16[96]{0:T(256)(128)(2,1)S(1)} all-reduce(bf16[96]{0:T(256)(128)(2,1)S(1)} %dynamic-update-slice), channel_id=1, replica_groups=mesh['req'=32,'head'=4] {'req'}, use_global_device_ids=true, to_apply=%add.1 | all-reduce | flops 96 | bytes 384
  75.6 25.6 %all-gather.1 = bf16[32,3,512]{2,1,0:T(4,128)(2,1)S(1)} all-gather(bf16[1,3,512]{2,1,0:T(4,128)(2,1)} %bitcast.118), channel_id=1, replica_groups=mesh['req'=32,'head'=4] {'req'}, dimensions={0}, use_global_device_ids=true | all-gather | bytes 101376 | tf_op jit(solution)/shard_map/all_gather | solution.py:156
  103.5 3.0 fusion.89
  108.5 3.1 fusion.88
  112.9 25.6 %all-gather = bf16[32,3,512]{2,1,0:T(4,128)(2,1)S(1)} all-gather(bf16[1,3,512]{2,1,0:T(4,128)(2,1)S(1)} %reshape.338), channel_id=1, replica_groups=mesh['req'=32,'head'=4] {'req'}, dimensions={0}, use_global_device_ids=true | all-gather | bytes 101376 | tf_op jit(solution)/shard_map/all_gather | solution.py:157
  138.9 1.8 multiply_cosine_fusion
  140.9 5.8 %fusion.87 = (bf16[3,1,2048,256]{3,2,1,0:T(8,128)(2,1)}, bf16[3,1,2048,256]{3,2,1,0:T(8,128)(2,1)}) fusion(bf16[3,2,2048,256]{3,2,1,0:T(8,128)(2,1)} %param.22), kind=kLoop, calls=%fused_computation.112 | loop fusion | bytes 12582912 | tf_op jit(solution)/shard_map/vmap()/slice | solution.py:97
  146.7 3.2 copy.81
  149.9 2.8 copy.73
  152.7 3.2 copy.80
  155.9 2.8 copy.71
  158.9 3.1 fusion.90
  162.9 22.5 %all-gather.2 = bf16[32,3,512]{2,1,0:T(4,128)(2,1)S(1)} all-gather(bf16[1,3,512]{2,1,0:T(4,128)(2,1)S(1)} %reshape.342), channel_id=1, replica_groups=mesh['req'=32,'head'=4] {'req'}, dimensions={0}, use_global_device_ids=true | all-gather | bytes 101376 | tf_op jit(solution)/shard_map/all_gather | solution.py:171
  185.7 2.0 pad_add_fusion
  190.5 2.3 copy.78
  192.9 2.3 copy.64
  195.1 2.4 copy.67
  199.0 2.3 copy.57
  201.3 1.9 copy.58
  203.4 12.7 %fusion.2 = (f32[2,2,512]{2,1,0:T(2,128)S(1)}, f32[2,2560,512,2]{2,1,3,0:T(8,128)}) fusion(pred[512,2560]{0,1:T(8,128)(4,1)S(1)} %pad_add_fusion, f32[512,2,2,64]{3,0,2,1:T(8,128)} %copy.68, f32[512,2,2,64]{3,0,2,1:T(8,128)} %copy.67, f32[512,2,2,128]{3,2,1,0:T(2,128)S(1)} %reshape.332, f32[512,128]{1,0:T(8,128)S(1)} %get-tuple-element.47, ...), kind=kOutput, calls=%fused_computation.4 | convolution fusion | flops 1361836032 | bytes 26222592 | tf_op jit(solution)/shard_map/while/body/eval_jaxpr/qhgd,khd->hgqk/dot_general | solution.py:35
  216.1 9.6 %fusion = f32[2,2,512]{2,1,0:T(2,128)S(1)} fusion(f32[2,2560,512,2]{2,1,3,0:T(8,128)} %get-tuple-element.43, f32[2,2,512]{2,1,0:T(2,128)S(1)} %get-tuple-element.42, pred[512,2560]{0,1:T(8,128)(4,1)S(1)} %pad_add_fusion), kind=kLoop, calls=%fused_computation.2 | loop fusion | flops 20969472 | bytes 22298624 | tf_op jit(solution)/shard_map/while/body/eval_jaxpr/reduce_sum | solution.py:41
  225.8 10.6 %fusion.28 = bf16[512,2,2,128]{0,3,2,1:T(8,128)(2,1)S(1)} fusion(f32[2,2560,512,2]{2,1,3,0:T(8,128)} %get-tuple-element.43, f32[2,2,512]{2,1,0:T(2,128)S(1)} %get-tuple-element.42, pred[512,2560]{0,1:T(8,128)(4,1)S(1)} %pad_add_fusion, bf16[512,2,128]{0,2,1:T(8,128)(2,1)S(1)} %bitcast.114, bf16[2048,2,128]{0,2,1:T(8,128)(2,1)S(1)} %bitcast.112, ...), kind=kOutput, calls=%fused_computation.32 | convolution fusion | flops 1366294528 | bytes 24133632 | tf_op jit(solution)/shard_map/while/body/eval_jaxpr/hgqk,khd->qhgd/dot_general | solution.py:43
  236.5 5.3 fusion.47
  241.8 2.5 add_dynamic-update-slice_fusion
  246.3 91.8 %all-reduce.4.cloned.1.call-done = f32[515,2048]{1,0:T(8,128)} async-done(((f32[515,2048]{1,0:T(8,128)}), f32[515,2048]{1,0:T(8,128)}) %all-reduce.4.cloned.1.call-update) | async-done | bytes 4218896 | tf_op jit(solution)/shard_map/psum | solution.py:193
  338.1 2.6 multiply_reduce_fusion
  340.7 48.8 %all-gather.10.cloned.1.call-done = bf16[2048,1536]{1,0:T(8,128)(2,1)} async-done(((bf16[64,1536]{1,0:T(8,128)(2,1)}), bf16[2048,1536]{1,0:T(8,128)(2,1)}) %all-gather.10.cloned.1.call-update) | async-done | bytes 6291472 | tf_op jit(solution)/shard_map/all_gather | solution.py:203
  389.5 7.0 %fusion.86 = f32[515,1536]{1,0:T(8,128)S(1)} fusion(bf16[2048,1536]{1,0:T(8,128)(2,1)} %all-gather.10.cloned.1.call-done, f32[515,2048]{1,0:T(8,128)} %all-reduce.4.cloned.1.call-done, f32[2048]{0:T(1024)S(1)} %convert_element_type.169, f32[515]{0:T(1024)S(1)} %add_rsqrt_fusion), kind=kOutput, calls=%fused_computation.111 | convolution fusion | flops 3243264000 | bytes 13684748 | tf_op jit(solution)/shard_map/dot_general | solution.py:201
  396.5 42.8 %all-gather.12.cloned.1.call-done = bf16[2048,1536]{1,0:T(8,128)(2,1)} async-done(((bf16[64,1536]{1,0:T(8,128)(2,1)}), bf16[2048,1536]{1,0:T(8,128)(2,1)}) %all-gather.12.cloned.1.call-update) | async-done | bytes 6291472 | tf_op jit(solution)/shard_map/all_gather | solution.py:204
  439.3 49.8 %all-gather.14.cloned.1.call-done = bf16[1536,2048]{0,1:T(8,128)(2,1)} async-done(((bf16[1536,64]{0,1:T(8,128)(2,1)}), bf16[1536,2048]{0,1:T(8,128)(2,1)}) %all-gather.14.cloned.1.call-update) | async-done | bytes 6291472 | tf_op jit(solution)/shard_map/all_gather | solution.py:208
  489.1 14.8 %fusion.46 = f32[515,2048]{1,0:T(8,128)} fusion(bf16[1536,2048]{0,1:T(8,128)(2,1)} %all-gather.14.cloned.1.call-done, bf16[2048,1536]{1,0:T(8,128)(2,1)} %all-gather.12.cloned.1.call-done, f32[515,1536]{1,0:T(8,128)S(1)} %fusion.86, f32[515,2048]{1,0:T(8,128)} %all-reduce.4.cloned.1.call-done, f32[2048]{0:T(1024)S(1)} %convert_element_type.169, ...), kind=kOutput, calls=%fused_computation.48 | convolution fusion | flops 6488110080 | bytes 24195084 | tf_op jit(solution)/shard_map/dot_general | solution.py:206
  503.9 46.1 %reduce-scatter.2.cloned.1.call-done = f32[515,512]{1,0:T(8,128)} async-done(((f32[515,2048]{1,0:T(8,128)}), f32[515,512]{1,0:T(8,128)}) %reduce-scatter.2.cloned.1.call-update) | async-done | bytes 1054736 | tf_op jit(solution)/shard_map/reduce_scatter | solution.py:212
  (95 shorter events, 20.0 us)
Async XLA Ops:
  7.2 229.3 %all-gather.8.cloned.1.call-start = ((), (), s32[]{:S(2)}) async-start(), calls=%async_computation.1 | async-start | bytes 2162688 | tf_op jit(solution)/shard_map/all_gather | solution.py:183
  7.9 330.2 %all-reduce.4.cloned.1.call-start = ((), (), s32[]{:S(2)}) async-start(), calls=%async_computation.2 | async-start | bytes 8519680 | tf_op jit(solution)/shard_map/psum | solution.py:193
  107.3 4.4 copy-start
  107.3 4.2 copy-start.3
  108.5 4.4 copy-start.15
  158.9 3.4 copy-start.2
  162.2 23.2 %copy-start.9 = (f32[512,64]{1,0:T(8,128)S(1)}, f32[512,64]{1,0:T(8,128)}, u32[]{:S(2)}) copy-start(f32[512,64]{1,0:T(8,128)} %get-tuple-element.36) | copy-start | bytes 393220
  162.2 23.2 %copy-start.10 = (f32[512,64]{1,0:T(8,128)S(1)}, f32[512,64]{1,0:T(8,128)}, u32[]{:S(2)}) copy-start(f32[512,64]{1,0:T(8,128)} %get-tuple-element.37) | copy-start | bytes 393220
  162.8 24.9 %copy-start.1 = (f32[512,2,128]{2,0,1:T(8,128)S(1)}, f32[512,2,128]{2,0,1:T(8,128)}, u32[]{:S(2)}) copy-start(f32[512,2,128]{2,0,1:T(8,128)} %copy-done) | copy-start | bytes 1572868
  162.8 24.9 %copy-start.5 = (f32[512,2,64]{2,0,1:T(8,128)S(1)}, f32[512,2,64]{2,0,1:T(8,128)}, u32[]{:S(2)}) copy-start(f32[512,2,64]{2,0,1:T(8,128)} %get-tuple-element.28) | copy-start | bytes 786436
  162.8 24.9 %copy-start.6 = (f32[512,2,64]{2,0,1:T(8,128)S(1)}, f32[512,2,64]{2,0,1:T(8,128)}, u32[]{:S(2)}) copy-start(f32[512,2,64]{2,0,1:T(8,128)} %get-tuple-element.29) | copy-start | bytes 786436
  162.9 25.8 %copy-start.16 = (s32[3]{0:T(128)S(1)}, s32[3]{0:T(128)}, u32[]{:S(2)}) copy-start(s32[3]{0:T(128)} %param.24) | copy-start | bytes 40
  190.5 7.1 %copy-start.4 = (f32[512,4,64]{0,2,1:T(8,128)S(1)}, f32[512,4,64]{0,2,1:T(8,128)}, u32[]{:S(2)}) copy-start(f32[512,4,64]{0,2,1:T(8,128)} %get-tuple-element.25) | copy-start | bytes 1572868
  199.0 4.4 copy-start.7
  216.1 9.6 %copy-start.8 = (bf16[1,1,2048,256]{2,3,1,0:T(8,128)(2,1)S(1)}, bf16[1,1,2048,256]{2,3,1,0:T(8,128)(2,1)}, u32[]{:S(2)}) copy-start(bf16[1,1,2048,256]{2,3,1,0:T(8,128)(2,1)} %copy.57) | copy-start | bytes 3145732
  216.1 9.6 %copy-start.12 = (bf16[512,1,256]{0,2,1:T(8,128)(2,1)S(1)}, bf16[512,1,256]{0,2,1:T(8,128)(2,1)}, u32[]{:S(2)}) copy-start(bf16[512,1,256]{0,2,1:T(8,128)(2,1)} %copy.58) | copy-start | bytes 786436
  236.4 5.3 copy-start.11
  236.5 5.3 copy-start.13
  241.8 4.5 copy-start.14
  244.3 145.2 %all-gather.10.cloned.1.call-start = ((), (), s32[]{:S(2)}) async-start(), calls=%async_computation.3 | async-start | bytes 6488064 | tf_op jit(solution)/shard_map/all_gather | solution.py:203
  245.0 194.3 %all-gather.12.cloned.1.call-start = ((), (), s32[]{:S(2)}) async-start(), calls=%async_computation.4 | async-start | bytes 6488064 | tf_op jit(solution)/shard_map/all_gather | solution.py:204
  245.6 243.5 %all-gather.14.cloned.1.call-start = ((), (), s32[]{:S(2)}) async-start(), calls=%async_computation.5 | async-start | bytes 6488064 | tf_op jit(solution)/shard_map/all_gather | solution.py:208
  246.2 303.9 %reduce-scatter.2.cloned.1.call-start = ((), (), s32[]{:S(2)}) async-start(), calls=%async_computation.6 | async-start | bytes 5324800 | tf_op jit(solution)/shard_map/reduce_scatter | solution.py:212
Sparse Core Ops, SparseCore 0:
  10.2 47.0 all-gather.7
  244.4 93.6 all-reduce.3
  340.4 49.0 all-gather.9
  391.6 47.6 all-gather.11
  441.4 47.6 all-gather.13
  504.0 45.9 reduce-scatter.1
where the time goes:
time: 561 us; the launch traced here: 560 us
  waiting for transfers between devices  282 us (50%)
  blocking collectives  138 us (25%)
  matrix products  54.7 us (10%)
  local copies, waits for them, and re-layouts  42.7 us (8%)
  other arithmetic  27.1 us (5%)
  between operations  15.7 us (3%)
    psum x1, waiting for transfers between devices, body(): summed_full = lax.psum(placed, 'head')  91.8 us
    unnamed x1, blocking collectives  64.1 us
    all_gather x1, waiting for transfers between devices, body(): lax.all_gather(down_weight, 'req', axis=1, tiled=True)  49.8 us
    all_gather x1, waiting for transfers between devices, body(): gate_sum = add_rows(lax.all_gather(gate_weight, 'req', axis=0, tiled=True))  48.8 us
    reduce_scatter x1, waiting for transfers between devices, body(): lax.psum_scatter(down_terms, 'head', scatter_dimension=1, tiled=True)  46.1 us
    all_gather x1, waiting for transfers between devices, body(): upper = add_rows(lax.all_gather(up_weight, 'req', axis=0, tiled=True))  42.8 us
    all_gather x1, blocking collectives, body(): lax.all_gather(fresh_flat, 'req', axis=0, tiled=True)  25.6 us
    all_gather x1, blocking collectives, body(): lax.all_gather(decode_query, 'req', axis=0, tiled=True)  25.6 us
  transfers between devices with their start and end apart: 6, of which 5 were waited for; matrix products, arithmetic and copies ran while one was open for 18% of the time, Pallas kernels for 0%

commit v1 on v0

--- a/solution.py
+++ b/solution.py
@@ -203,11 +203,10 @@
     gate_sum = add_rows(lax.all_gather(gate_weight, "req", axis=0, tiled=True))
     upper = add_rows(lax.all_gather(up_weight, "req", axis=0, tiled=True))
     hidden = (jax.nn.silu(gate_sum) * upper).astype(jnp.bfloat16)
-    down_terms = jnp.dot(
-        hidden,
-        lax.all_gather(down_weight, "req", axis=1, tiled=True),
-        preferred_element_type=jnp.float32,
-    )
+    feed_sample = lambda x_in: jnp.concatenate(
+        lax.all_to_all(jnp.stack([x_in for _ in range(lax.axis_size("req"))], 0), "req", 0, 0), 1
+    )
+    down_terms = jnp.dot(hidden, feed_sample(down_weight), preferred_element_type=jnp.float32)
     result = (
         summed + lax.psum_scatter(down_terms, "head", scatter_dimension=1, tiled=True)
     ).astype(jnp.bfloat16)

time: 561 us -> 511 us (0.911)
  waiting for transfers between devices: 282 us -> 224 us
    all_gather x1 -> x0, waiting for transfers between devices: 49.8 us -> none  [body(): lax.all_gather(down_weight, 'req', axis=1, tiled=True)]
    psum x1, waiting for transfers between devices: 91.8 us -> 84 us  [body(): summed_full = lax.psum(placed, 'head')]
    unnamed x46 -> x48, local copies, waits for them, and re-layouts: 11.3 us -> 11.3 us
  transfers between devices with their start and end apart: 6 -> 6, of which waited for: 5 -> 4; matrix products, arithmetic and copies ran while one was open for 18% -> 20% of each run, Pallas kernels for 0% -> 0%
where the time goes in v1:
time: 511 us; the launch traced here: 510 us
  waiting for transfers between devices  224 us (44%)
  blocking collectives  138 us (27%)
  matrix products  54.6 us (11%)
  local copies, waits for them, and re-layouts  46.3 us (9%)
  other arithmetic  27 us (5%)
  between operations  15.4 us (3%)
  starting transfers between devices  5.41 us (1%)
    psum x1, waiting for transfers between devices, body(): summed_full = lax.psum(placed, 'head')  84 us
    unnamed x1, blocking collectives  64.1 us
    all_gather x1, waiting for transfers between devices, body(): gate_sum = add_rows(lax.all_gather(gate_weight, 'req', axis=0, tiled=True))  48.8 us
    reduce_scatter x1, waiting for transfers between devices, body(): lax.psum_scatter(down_terms, 'head', scatter_dimension=1, tiled=True)  46.1 us
    all_gather x1, waiting for transfers between devices, body(): upper = add_rows(lax.all_gather(up_weight, 'req', axis=0, tiled=True))  42.8 us
    all_gather x1, blocking collectives, body(): lax.all_gather(fresh_flat, 'req', axis=0, tiled=True)  25.6 us
    all_gather x1, blocking collectives, body(): lax.all_gather(decode_query, 'req', axis=0, tiled=True)  25.6 us
    all_gather x1, blocking collectives, body(): every_att = lax.all_gather(own_att, 'req', axis=0, tiled=True)  22.5 us
  transfers between devices with their start and end apart: 6, of which 4 were waited for; matrix products, arithmetic and copies ran while one was open for 20% of the time, Pallas kernels for 0%

profile of v1, /device:TPU:1, one launch (start us, length us, event | category | flops | bytes accessed | tf_op | source)
XLA Modules:
  0.0 510.1 jit_solution(5682497568819913233)
XLA Ops:
  11.5 64.1 %all-reduce.1 = bf16[96]{0:T(256)(128)(2,1)S(1)} all-reduce(bf16[96]{0:T(256)(128)(2,1)S(1)} %dynamic-update-slice), channel_id=1, replica_groups=mesh['req'=32,'head'=4] {'req'}, use_global_device_ids=true, to_apply=%add.1 | all-reduce | flops 96 | bytes 384
  75.6 25.6 %all-gather.1 = bf16[32,3,512]{2,1,0:T(4,128)(2,1)S(1)} all-gather(bf16[1,3,512]{2,1,0:T(4,128)(2,1)} %bitcast.121), channel_id=1, replica_groups=mesh['req'=32,'head'=4] {'req'}, dimensions={0}, use_global_device_ids=true | all-gather | bytes 101376 | tf_op jit(solution)/shard_map/all_gather | solution.py:156
  103.5 3.1 fusion.89
  108.7 3.1 fusion.88
  113.1 25.6 %all-gather = bf16[32,3,512]{2,1,0:T(4,128)(2,1)S(1)} all-gather(bf16[1,3,512]{2,1,0:T(4,128)(2,1)S(1)} %reshape.348), channel_id=1, replica_groups=mesh['req'=32,'head'=4] {'req'}, dimensions={0}, use_global_device_ids=true | all-gather | bytes 101376 | tf_op jit(solution)/shard_map/all_gather | solution.py:157
  141.1 5.8 %fusion.87 = (bf16[3,1,2048,256]{3,2,1,0:T(8,128)(2,1)}, bf16[3,1,2048,256]{3,2,1,0:T(8,128)(2,1)}) fusion(bf16[3,2,2048,256]{3,2,1,0:T(8,128)(2,1)} %param.22), kind=kLoop, calls=%fused_computation.112 | loop fusion | bytes 12582912 | tf_op jit(solution)/shard_map/vmap()/slice | solution.py:97
  146.9 3.2 copy.82
  150.1 2.8 copy.74
  152.9 3.2 copy.81
  156.1 2.8 copy.72
  159.1 3.1 fusion.90
  163.1 22.5 %all-gather.2 = bf16[32,3,512]{2,1,0:T(4,128)(2,1)S(1)} all-gather(bf16[1,3,512]{2,1,0:T(4,128)(2,1)S(1)} %reshape.352), channel_id=1, replica_groups=mesh['req'=32,'head'=4] {'req'}, dimensions={0}, use_global_device_ids=true | all-gather | bytes 101376 | tf_op jit(solution)/shard_map/all_gather | solution.py:171
  185.9 2.0 pad_add_fusion
  190.7 2.3 copy.79
  193.1 2.3 copy.65
  195.3 2.4 copy.68
  199.2 2.3 copy.58
  201.5 1.9 copy.59
  203.6 12.7 %fusion.2 = (f32[2,2,512]{2,1,0:T(2,128)S(1)}, f32[2,2560,512,2]{2,1,3,0:T(8,128)}) fusion(pred[512,2560]{0,1:T(8,128)(4,1)S(1)} %pad_add_fusion, f32[512,2,2,64]{3,0,2,1:T(8,128)} %copy.69, f32[512,2,2,64]{3,0,2,1:T(8,128)} %copy.68, f32[512,2,2,128]{3,2,1,0:T(2,128)S(1)} %reshape.342, f32[512,128]{1,0:T(8,128)S(1)} %get-tuple-element.47, ...), kind=kOutput, calls=%fused_computation.4 | convolution fusion | flops 1361836032 | bytes 26222592 | tf_op jit(solution)/shard_map/while/body/eval_jaxpr/qhgd,khd->hgqk/dot_general | solution.py:35
  216.3 9.6 %fusion = f32[2,2,512]{2,1,0:T(2,128)S(1)} fusion(f32[2,2560,512,2]{2,1,3,0:T(8,128)} %get-tuple-element.43, f32[2,2,512]{2,1,0:T(2,128)S(1)} %get-tuple-element.42, pred[512,2560]{0,1:T(8,128)(4,1)S(1)} %pad_add_fusion), kind=kLoop, calls=%fused_computation.2 | loop fusion | flops 20969472 | bytes 22298624 | tf_op jit(solution)/shard_map/while/body/eval_jaxpr/reduce_sum | solution.py:41
  225.9 10.6 %fusion.28 = bf16[512,2,2,128]{0,3,2,1:T(8,128)(2,1)S(1)} fusion(f32[2,2560,512,2]{2,1,3,0:T(8,128)} %get-tuple-element.43, f32[2,2,512]{2,1,0:T(2,128)S(1)} %get-tuple-element.42, pred[512,2560]{0,1:T(8,128)(4,1)S(1)} %pad_add_fusion, bf16[512,2,128]{0,2,1:T(8,128)(2,1)S(1)} %bitcast.117, bf16[2048,2,128]{0,2,1:T(8,128)(2,1)S(1)} %bitcast.115, ...), kind=kOutput, calls=%fused_computation.32 | convolution fusion | flops 1366294528 | bytes 24133632 | tf_op jit(solution)/shard_map/while/body/eval_jaxpr/hgqk,khd->qhgd/dot_general | solution.py:43
  236.6 5.2 %fusion.47 = f32[515,2048]{1,0:T(8,128)} fusion(bf16[512,2048]{0,1:T(8,128)(2,1)} %all-gather.7.cloned.1.call-done, bf16[3,512]{0,1:T(8,128)(2,1)S(1)} %copy.75, bf16[512,512]{0,1:T(8,128)(2,1)S(1)} %bitcast.116), kind=kOutput, calls=%fused_computation.49 | convolution fusion | flops 1081088000 | bytes 6843392 | tf_op jit(solution)/shard_map/dot_general | solution.py:181
  241.9 2.4 add_dynamic-update-slice_fusion
  245.7 3.3 stack.2
  249.0 5.2 %all-to-all-start = ((bf16[32,1536,64]{1,2,0:T(8,128)(2,1)}), bf16[32,1536,64]{1,2,0:T(8,128)(2,1)}, u32[]{:S(2)}, u32[]{:S(2)}) async-start(bf16[32,1536,64]{1,2,0:T(8,128)(2,1)} %stack.2), calls=%async_computation | async-start | bytes 12582912 | tf_op jit(solution)/shard_map/all_to_all | solution.py:207
  254.3 84.0 %all-reduce.4.cloned.1.call-done = f32[515,2048]{1,0:T(8,128)} async-done(((f32[515,2048]{1,0:T(8,128)}), f32[515,2048]{1,0:T(8,128)}) %all-reduce.4.cloned.1.call-update) | async-done | bytes 4218896 | tf_op jit(solution)/shard_map/psum | solution.py:193
  338.3 2.6 multiply_reduce_fusion
  340.8 48.8 %all-gather.9.cloned.1.call-done = bf16[2048,1536]{1,0:T(8,128)(2,1)} async-done(((bf16[64,1536]{1,0:T(8,128)(2,1)}), bf16[2048,1536]{1,0:T(8,128)(2,1)}) %all-gather.9.cloned.1.call-update) | async-done | bytes 6291472 | tf_op jit(solution)/shard_map/all_gather | solution.py:203
  389.7 7.0 %fusion.86 = f32[515,1536]{1,0:T(8,128)S(1)} fusion(bf16[2048,1536]{1,0:T(8,128)(2,1)} %all-gather.9.cloned.1.call-done, f32[515,2048]{1,0:T(8,128)} %all-reduce.4.cloned.1.call-done, f32[2048]{0:T(1024)S(1)} %convert_element_type.169, f32[515]{0:T(1024)S(1)} %add_rsqrt_fusion), kind=kOutput, calls=%fused_computation.111 | convolution fusion | flops 3243264000 | bytes 13684748 | tf_op jit(solution)/shard_map/dot_general | solution.py:201
  396.7 42.8 %all-gather.11.cloned.1.call-done = bf16[2048,1536]{1,0:T(8,128)(2,1)} async-done(((bf16[64,1536]{1,0:T(8,128)(2,1)}), bf16[2048,1536]{1,0:T(8,128)(2,1)}) %all-gather.11.cloned.1.call-update) | async-done | bytes 6291472 | tf_op jit(solution)/shard_map/all_gather | solution.py:204
  439.5 14.8 %fusion.46 = f32[515,2048]{1,0:T(8,128)} fusion(bf16[1536,2048]{0,1:T(8,128)(2,1)} %bitcast.37, bf16[2048,1536]{1,0:T(8,128)(2,1)} %all-gather.11.cloned.1.call-done, f32[515,1536]{1,0:T(8,128)S(1)} %fusion.86, f32[515,2048]{1,0:T(8,128)} %all-reduce.4.cloned.1.call-done, f32[2048]{0:T(1024)S(1)} %convert_element_type.169, f32[515]{0:T(1024)S(1)} %add_rsqrt_fusion), kind=kOutput, calls=%fused_computation.48 | convolution fusion | flops 6488110080 | bytes 24195084 | tf_op jit(solution)/shard_map/dot_general | solution.py:209
  454.3 46.1 %reduce-scatter.2.cloned.1.call-done = f32[515,512]{1,0:T(8,128)} async-done(((f32[515,2048]{1,0:T(8,128)}), f32[515,512]{1,0:T(8,128)}) %reduce-scatter.2.cloned.1.call-update) | async-done | bytes 1054736 | tf_op jit(solution)/shard_map/reduce_scatter | solution.py:211
  (97 shorter events, 21.3 us)
Async XLA Ops:
  7.2 229.5 %all-gather.7.cloned.1.call-start = ((), (), s32[]{:S(2)}) async-start(), calls=%async_computation.2 | async-start | bytes 2162688 | tf_op jit(solution)/shard_map/all_gather | solution.py:183
  7.9 330.4 %all-reduce.4.cloned.1.call-start = ((), (), s32[]{:S(2)}) async-start(), calls=%async_computation.3 | async-start | bytes 8519680 | tf_op jit(solution)/shard_map/psum | solution.py:193
  107.5 4.4 copy-start
  107.5 4.2 copy-start.3
  108.7 4.4 copy-start.16
  159.1 3.4 copy-start.2
  162.4 23.2 %copy-start.9 = (f32[512,64]{1,0:T(8,128)S(1)}, f32[512,64]{1,0:T(8,128)}, u32[]{:S(2)}) copy-start(f32[512,64]{1,0:T(8,128)} %get-tuple-element.36) | copy-start | bytes 393220
  162.4 23.2 %copy-start.10 = (f32[512,64]{1,0:T(8,128)S(1)}, f32[512,64]{1,0:T(8,128)}, u32[]{:S(2)}) copy-start(f32[512,64]{1,0:T(8,128)} %get-tuple-element.37) | copy-start | bytes 393220
  163.0 24.9 %copy-start.1 = (f32[512,2,128]{2,0,1:T(8,128)S(1)}, f32[512,2,128]{2,0,1:T(8,128)}, u32[]{:S(2)}) copy-start(f32[512,2,128]{2,0,1:T(8,128)} %copy-done) | copy-start | bytes 1572868
  163.0 24.9 %copy-start.5 = (f32[512,2,64]{2,0,1:T(8,128)S(1)}, f32[512,2,64]{2,0,1:T(8,128)}, u32[]{:S(2)}) copy-start(f32[512,2,64]{2,0,1:T(8,128)} %get-tuple-element.28) | copy-start | bytes 786436
  163.0 24.9 %copy-start.6 = (f32[512,2,64]{2,0,1:T(8,128)S(1)}, f32[512,2,64]{2,0,1:T(8,128)}, u32[]{:S(2)}) copy-start(f32[512,2,64]{2,0,1:T(8,128)} %get-tuple-element.29) | copy-start | bytes 786436
  163.0 25.8 %copy-start.17 = (s32[3]{0:T(128)S(1)}, s32[3]{0:T(128)}, u32[]{:S(2)}) copy-start(s32[3]{0:T(128)} %param.24) | copy-start | bytes 40
  190.7 7.1 %copy-start.4 = (f32[512,4,64]{0,2,1:T(8,128)S(1)}, f32[512,4,64]{0,2,1:T(8,128)}, u32[]{:S(2)}) copy-start(f32[512,4,64]{0,2,1:T(8,128)} %get-tuple-element.25) | copy-start | bytes 1572868
  199.2 4.4 copy-start.7
  216.3 9.6 %copy-start.8 = (bf16[1,1,2048,256]{2,3,1,0:T(8,128)(2,1)S(1)}, bf16[1,1,2048,256]{2,3,1,0:T(8,128)(2,1)}, u32[]{:S(2)}) copy-start(bf16[1,1,2048,256]{2,3,1,0:T(8,128)(2,1)} %copy.58) | copy-start | bytes 3145732
  216.3 9.6 %copy-start.12 = (bf16[512,1,256]{0,2,1:T(8,128)(2,1)S(1)}, bf16[512,1,256]{0,2,1:T(8,128)(2,1)}, u32[]{:S(2)}) copy-start(bf16[512,1,256]{0,2,1:T(8,128)(2,1)} %copy.59) | copy-start | bytes 786436
  236.6 5.3 %copy-start.11 = (bf16[512,512]{1,0:T(8,128)(2,1)S(1)}, bf16[512,512]{1,0:T(8,128)(2,1)}, u32[]{:S(2)}) copy-start(bf16[512,512]{1,0:T(8,128)(2,1)} %param.25) | copy-start | bytes 1572868
  236.6 5.2 %copy-start.14 = (bf16[3,512]{1,0:T(4,128)(2,1)S(1)}, bf16[3,512]{1,0:T(4,128)(2,1)}, u32[]{:S(2)}) copy-start(bf16[3,512]{1,0:T(4,128)(2,1)} %param.26) | copy-start | bytes 9220
  241.9 3.8 copy-start.13
  244.3 145.3 %all-gather.9.cloned.1.call-start = ((), (), s32[]{:S(2)}) async-start(), calls=%async_computation.4 | async-start | bytes 6488064 | tf_op jit(solution)/shard_map/all_gather | solution.py:203
  245.1 194.4 %all-gather.11.cloned.1.call-start = ((), (), s32[]{:S(2)}) async-start(), calls=%async_computation.5 | async-start | bytes 6488064 | tf_op jit(solution)/shard_map/all_gather | solution.py:204
  249.0 5.3 %copy-start.15 = (bf16[2048]{0:T(1024)(128)(2,1)S(1)}, bf16[2048]{0:T(1024)(128)(2,1)}, u32[]{:S(2)}) copy-start(bf16[2048]{0:T(1024)(128)(2,1)} %param.28) | copy-start | bytes 12292
  249.0 147.7 %all-to-all-start = ((bf16[32,1536,64]{1,2,0:T(8,128)(2,1)}), bf16[32,1536,64]{1,2,0:T(8,128)(2,1)}, u32[]{:S(2)}, u32[]{:S(2)}) async-start(bf16[32,1536,64]{1,2,0:T(8,128)(2,1)} %stack.2), calls=%async_computation | async-start | bytes 12582912 | tf_op jit(solution)/shard_map/all_to_all | solution.py:207
  254.2 246.2 %reduce-scatter.2.cloned.1.call-start = ((), (), s32[]{:S(2)}) async-start(), calls=%async_computation.6 | async-start | bytes 5324800 | tf_op jit(solution)/shard_map/reduce_scatter | solution.py:211
Sparse Core Ops, SparseCore 0:
  10.2 47.0 all-gather.6
  244.5 93.7 all-reduce.3
  340.5 49.0 all-gather.8
  391.8 47.6 all-gather.10
  454.4 45.9 reduce-scatter.1
